TPU v7x, 32 devices: a whole 2x2x4 slice. The times are simulated.
32 devices in a mesh: groups: 2 (over y), seq: 16 (over z, x, core).
Axes of the slice: x: 2, y: 2, z: 4, core: 2. Of those that a mesh axis runs over, the one named last changes fastest.
Arguments:
- bases: int32 [8192], P(('groups', 'seq')), parts along dimension 0, may hold values from 0 to 3
- base_table: bfloat16 [4, 768], replicated, may hold values from -4 to 4
- first_kernel: bfloat16 [768, 864], P('seq'), may hold values from -0.21875 to 0.21875
- second_kernel: bfloat16 [768, 864], P('seq'), may hold values from -0.21875 to 0.21875
- cotangent: bfloat16 [8192, 768], P(('groups', 'seq')), parts along dimension 0, may hold values from -0.125 to 0.125
Outputs:
- combined: bfloat16 [8192, 768], P(('groups', 'seq')), parts along dimension 0
- first_grad: float32 [1536, 864], P(('groups', 'seq')), parts along dimension 0
- second_grad: float32 [1536, 864], P(('groups', 'seq')), parts along dimension 0
There are 2 independent parts, one for each index of `groups`. A program takes and returns all parts, laid end to end along the dimension named above; an argument that names none is the same for every part. Nothing has to cross between parts.
Inputs may be any that keep to these rules, and one draw needn't show every extreme that they name: `bases`: base codes; the complement of code b is 3 - b.
All inputs are finite; a program needn't handle non-finite values.
Results may differ from a plain program's by a relative error of at most 0.0044.
Values may be sent and summed in bfloat16 or wider, within the bound.
A program may use at most 128 MiB of HBM per device.

v0:
```python
import jax
import jax.numpy as jnp
from jax import lax
from jax.sharding import PartitionSpec as P

GROUPS = 8
TAPS = 9


def from_partner(block, axis, apart):
    count = lax.axis_size(axis)
    route = []
    for low in range(count):
        high = low | 1 << apart
        if high != low and high < count:
            route += [(low, high), (high, low)]
    return lax.ppermute(block, axis, route)


def extended_2(cells, sides, width):
    for axis, dim in sides:
        count = lax.axis_size(axis)
        ends = count - 1
        head = lax.slice_in_dim(cells, 0, width, axis=dim)
        tail = lax.slice_in_dim(cells, cells.shape[dim] - width, cells.shape[dim], axis=dim)
        cells = jnp.concatenate(
            [
                lax.ppermute(tail, axis, [(i, (i + 1) % count) for i in range(ends)]),
                cells,
                lax.ppermute(head, axis, [((i + 1) % count, i) for i in range(ends)]),
            ],
            axis=dim,
        )
    return cells


def gelu_exact(values):
    return jax.nn.gelu(values, approximate=False)


def group_kernel(kernel, channels):
    group_width = channels // GROUPS
    return kernel.reshape(GROUPS, group_width, TAPS * group_width)


def adjoint_kernel(kernel):
    groups_count, group_width, width_all = kernel.shape
    flipped = kernel.reshape(groups_count, group_width, TAPS, group_width)[:, :, ::-1]
    return jnp.transpose(flipped, (0, 3, 2, 1)).reshape(groups_count, group_width, width_all)


def unfold(extended, out_rows):
    strands_count, _, channels = extended.shape
    group_width = channels // GROUPS
    pieces = extended.reshape(strands_count, -1, GROUPS, group_width)
    stacked = jnp.stack(
        [pieces[:, tap_index : tap_index + out_rows] for tap_index in range(TAPS)], axis=3
    )
    return stacked.reshape(strands_count, out_rows, GROUPS, TAPS * group_width)


def conv_cols(columns, kernels):
    strands_count, out_rows, _, _ = columns.shape
    summed = jnp.einsum("spgk,sgok->spgo", columns, kernels, preferred_element_type=jnp.float32)
    return summed.reshape(strands_count, out_rows, -1)


def correlate(grad_rows, columns):
    strands_count, band_rows, channels = grad_rows.shape
    grad_groups = grad_rows.reshape(strands_count, band_rows, GROUPS, channels // GROUPS)
    return jnp.einsum("spgo,spgk->sgok", grad_groups, columns, preferred_element_type=jnp.float32)


def per_device(bases, base_table, first_kernel, second_kernel, cotangent):
    band_rows = bases.shape[0]
    channels = base_table.shape[1]
    half_taps = TAPS // 2
    full_first, full_second = (
        lax.all_gather(first_kernel, "seq", axis=0, tiled=True),
        lax.all_gather(second_kernel, "seq", axis=0, tiled=True),
    )
    first_grouped = group_kernel(full_first, channels)
    second_grouped = group_kernel(full_second, channels)
    seq_count = lax.axis_size("seq")
    bit_count = seq_count.bit_length() - 1
    code_values = jnp.arange(4, dtype=jnp.int32)

    def embed_codes(code_rows):
        onehot = (code_rows[:, None] == code_values[None, :]).astype(jnp.bfloat16)
        return jnp.dot(onehot, base_table, preferred_element_type=jnp.float32).astype(jnp.bfloat16)

    partner = bases
    for flip_bit in range(bit_count):
        partner = from_partner(partner, "seq", flip_bit)
    second_in = embed_codes(3 - partner[::-1])
    first_kernels = jnp.stack([first_grouped, first_grouped])
    second_kernels = jnp.stack([second_grouped, second_grouped])
    cot_second = cotangent
    for flip_bit in range(bit_count):
        cot_second = from_partner(cot_second, "seq", flip_bit)
    cot_second = cot_second[::-1]
    strands = jnp.stack([embed_codes(bases), second_in])
    input_ext = extended_2(strands, (("seq", 1),), half_taps)
    input_cols = unfold(input_ext, band_rows)
    pre_act = conv_cols(input_cols, first_kernels)
    hidden = gelu_exact(pre_act).astype(jnp.bfloat16)
    hidden_ext = extended_2(hidden, (("seq", 1),), half_taps)
    hidden_cols = unfold(hidden_ext, band_rows)
    strand_out = strands.astype(jnp.float32) + conv_cols(hidden_cols, second_kernels)
    returned = strand_out[1].astype(jnp.bfloat16)
    for flip_bit in range(bit_count):
        returned = from_partner(returned, "seq", flip_bit)
    returned = returned[::-1]
    returned = lax.optimization_barrier(returned)
    combined = (strand_out[0] + returned.astype(jnp.float32)).astype(jnp.bfloat16)
    cotangent_stack = jnp.stack([cotangent, cot_second])
    cotangent_ext = extended_2(cotangent_stack, (("seq", 1),), half_taps)
    adjoint_kernels = jnp.stack(
        [adjoint_kernel(second_kernels[0]), adjoint_kernel(second_kernels[1])]
    )
    hidden_grad = conv_cols(unfold(cotangent_ext, band_rows), adjoint_kernels)
    _, pullback = jax.vjp(gelu_exact, pre_act)
    pre_grad = pullback(hidden_grad)[0].astype(jnp.bfloat16)
    second_terms = correlate(cotangent_stack, hidden_cols)
    first_terms = correlate(pre_grad, input_cols)
    first_local = first_terms[0] + first_terms[1]
    second_local = second_terms[0] + second_terms[1]
    first_grad, second_grad = (
        lax.psum_scatter(first_local.reshape(channels, -1), "seq", scatter_dimension=0, tiled=True),
        lax.psum_scatter(
            second_local.reshape(channels, -1), "seq", scatter_dimension=0, tiled=True
        ),
    )
    return (combined, first_grad, second_grad)


def solution(mesh):
    return jax.shard_map(
        per_device,
        mesh=mesh,
        in_specs=(
            P(("groups", "seq")),
            P(),
            P("seq", None),
            P("seq", None),
            P(("groups", "seq"), None),
        ),
        out_specs=(
            P(("groups", "seq"), None),
            P(("groups", "seq"), None),
            P(("groups", "seq"), None),
        ),
        check_vma=False,
    )
```

profile of v0, /device:TPU:1, one launch (start us, length us, event | category | flops | bytes accessed | tf_op | source)
XLA Modules:
  0.0 287.7 jit_solution(16473275754833019652)
XLA Ops:
  8.1 1.3 collective-permute-done
  9.4 2.4 collective-permute-start.1
  12.7 1.5 collective-permute-start.2
  14.3 1.0 collective-permute-done.2
  15.2 2.5 collective-permute-start.3
  17.7 1.0 fusion.51
  19.2 6.8 %collective-permute-start.4 = (bf16[2,4,768]{2,1,0:T(4,128)(2,1)S(1)}, bf16[2,4,768]{2,1,0:T(4,128)(2,1)S(1)}, u32[]{:S(2)}, u32[]{:S(2)}) collective-permute-start(bf16[2,4,768]{2,1,0:T(4,128)(2,1)S(1)} %get-tuple-element.9), channel_id=1, source_target_pairs={{0,1},{1,2},{2,3},{3,4},{4,5},{5,6},{6,7},{7,8},{8,9},{9,10},{10,1... | collective-permute-start | bytes 36872 | tf_op jit(solution)/shard_map/ppermute | solution.py:28
  26.0 1.9 collective-permute-start.5
  28.1 3.3 %collective-permute-done.5 = bf16[2,4,768]{2,1,0:T(4,128)(2,1)S(1)} collective-permute-done((bf16[2,4,768]{2,1,0:T(4,128)(2,1)S(1)}, bf16[2,4,768]{2,1,0:T(4,128)(2,1)S(1)}, u32[]{:S(2)}, u32[]{:S(2)}) %collective-permute-start.5) | collective-permute-done | bytes 12320 | tf_op jit(solution)/shard_map/ppermute | solution.py:30
  31.6 1.1 reshape.51
  32.7 1.1 fusion.61
  33.8 1.0 fusion.60
  34.8 1.9 collective-permute-start.13
  36.8 1.1 fusion.59
  37.8 1.1 fusion.58
  38.9 9.2 %collective-permute-done.13 = bf16[256,768]{1,0:T(8,128)(2,1)S(1)} collective-permute-done((bf16[256,768]{1,0:T(8,128)(2,1)S(1)}, bf16[256,768]{1,0:T(8,128)(2,1)S(1)}, u32[]{:S(2)}, u32[]{:S(2)}) %collective-permute-start.13) | collective-permute-done | bytes 393248 | tf_op jit(solution)/shard_map/ppermute | solution.py:17
  48.1 2.9 collective-permute-start.14
  50.9 1.1 fusion.57
  52.0 1.1 fusion.56
  53.1 7.7 %collective-permute-done.14 = bf16[256,768]{1,0:T(8,128)(2,1)S(1)} collective-permute-done((bf16[256,768]{1,0:T(8,128)(2,1)S(1)}, bf16[256,768]{1,0:T(8,128)(2,1)S(1)}, u32[]{:S(2)}, u32[]{:S(2)}) %collective-permute-start.14) | collective-permute-done | bytes 393248 | tf_op jit(solution)/shard_map/ppermute | solution.py:17
  60.8 1.4 collective-permute-start.15
  62.2 1.0 fusion.55
  63.2 1.2 fusion.54
  64.4 18.9 %collective-permute-done.15 = bf16[256,768]{1,0:T(8,128)(2,1)S(1)} collective-permute-done((bf16[256,768]{1,0:T(8,128)(2,1)S(1)}, bf16[256,768]{1,0:T(8,128)(2,1)S(1)}, u32[]{:S(2)}, u32[]{:S(2)}) %collective-permute-start.15) | collective-permute-done | bytes 393248 | tf_op jit(solution)/shard_map/ppermute | solution.py:17
  83.8 3.0 %collective-permute-start.16 = (bf16[2,4,768]{2,1,0:T(4,128)(2,1)S(1)}, bf16[2,4,768]{2,1,0:T(4,128)(2,1)S(1)}, u32[]{:S(2)}, u32[]{:S(2)}) collective-permute-start(bf16[2,4,768]{2,1,0:T(4,128)(2,1)S(1)} %get-tuple-element.5), channel_id=1, source_target_pairs={{0,1},{1,2},{2,3},{3,4},{4,5},{5,6},{6,7},{7,8},{8,9},{9,10},{10,1... | collective-permute-start | bytes 36872 | tf_op jit(solution)/shard_map/ppermute | solution.py:28
  86.7 1.9 collective-permute-start.17
  88.7 1.0 fusion.53
  89.7 12.2 %copy.30 = bf16[2,256,8,9,96]{1,4,3,2,0:T(8,128)(2,1)} copy(bf16[2,256,8,9,96]{4,2,1,0,3:T(8,128)(2,1)} %fusion.53) | data formatting | bytes 14155776 | tf_op jit(solution)/shard_map/stack | solution.py:56
  102.8 1.0 fusion.75
  103.8 1.2 fusion.74
  105.1 1.2 fusion.73
  106.3 1.2 fusion.72
  107.6 1.2 fusion.71
  108.8 1.3 fusion.70
  110.1 1.2 fusion.69
  111.3 1.3 fusion.68
  112.6 1.2 fusion.67
  113.8 1.8 copy.40
  115.6 1.9 reshape_squeeze_stack_reshape.4
  117.7 1.3 copy.41
  119.0 1.6 copy.42
  120.6 6.6 %negate_multiply_fusion = (f32[2,8,96,256]{3,2,1,0:T(8,128)S(1)}, f32[2,8,96,256]{3,2,1,0:T(8,128)}, f32[2,8,96,256]{3,2,1,0:T(8,128)S(1)}) fusion(bf16[2,256,8,864]{1,3,2,0:T(8,128)(2,1)} %bitcast.317, bf16[1,8,96,864]{3,2,1,0:T(8,128)(2,1)} %bitcast.331), kind=kOutput, calls=%fused_computation.63 | convolution fusion | flops 681984000 | bytes 13123584 | tf_op jit(solution)/shard_map/spgk,sgok->spgo/dot_general | solution.py:64
  127.2 14.6 %fusion.65 = f32[2,8,96,864]{3,2,1,0:T(8,128)} fusion(bf16[2,256,8,864]{1,3,2,0:T(8,128)(2,1)} %bitcast.318, bf16[2,256,8,864]{1,3,2,0:T(8,128)(2,1)} %bitcast.55, bf16[1,8,96,864]{3,2,1,0:T(8,128)(2,1)} %copy.42, f32[2,8,96,256]{3,2,1,0:T(8,128)S(1)} %get-tuple-element.11), kind=kOutput, calls=%fused_computation.95 | convolution fusion | flops 1388593152 | bytes 22364160 | tf_op jit(solution)/shard_map/spgo,spgk->sgok/dot_general | solution.py:71
  141.8 4.5 %slice_add_fusion.1 = f32[1,8,96,864]{3,2,1,0:T(8,128)} fusion(f32[2,8,96,864]{3,2,1,0:T(8,128)} %fusion.65), kind=kLoop, calls=%fused_computation.1 | loop fusion | flops 663552 | bytes 7962624 | tf_op jit(solution)/shard_map/add | solution.py:126
  146.3 4.4 %fusion.14 = bf16[2,256,768]{1,2,0:T(8,128)(2,1)S(1)} fusion(f32[2,8,96,256]{3,2,1,0:T(8,128)} %get-tuple-element.4, f32[2,8,96,256]{3,2,1,0:T(8,128)S(1)} %get-tuple-element.3), kind=kLoop, calls=%fused_computation.19 | loop fusion | flops 24379392 | bytes 3932160 | tf_op jit(solution)/shard_map/convert_element_type | solution.py:106
  151.0 3.8 %collective-permute-start.6 = (bf16[2,4,768]{1,2,0:T(8,128)(2,1)S(1)}, bf16[2,4,768]{1,2,0:T(8,128)(2,1)S(1)}, u32[]{:S(2)}, u32[]{:S(2)}) collective-permute-start(bf16[2,4,768]{1,2,0:T(8,128)(2,1)S(1)} %get-tuple-element.7), channel_id=1, source_target_pairs={{0,1},{1,2},{2,3},{3,4},{4,5},{5,6},{6,7},{7,8},{8,9},{9,10},{10,1... | collective-permute-start | bytes 36872 | tf_op jit(solution)/shard_map/ppermute | solution.py:28
  154.8 2.1 collective-permute-start.7
  157.3 2.2 collective-permute-done.6
  159.5 4.4 %collective-permute-done.7 = bf16[2,4,768]{1,2,0:T(8,128)(2,1)S(1)} collective-permute-done((bf16[2,4,768]{1,2,0:T(8,128)(2,1)S(1)}, bf16[2,4,768]{1,2,0:T(8,128)(2,1)S(1)}, u32[]{:S(2)}, u32[]{:S(2)}) %collective-permute-start.7) | collective-permute-done | bytes 12320 | tf_op jit(solution)/shard_map/ppermute | solution.py:30
  167.5 2.1 fusion.87
  170.4 1.9 slice_add_fusion
  172.2 1.3 copy-done.12
  173.6 5.6 %fusion = f32[2,8,96,256]{3,2,1,0:T(8,128)} fusion(bf16[2,256,8,864]{1,3,2,0:T(8,128)(2,1)} %bitcast.322, bf16[1,8,96,864]{3,2,1,0:T(8,128)(2,1)S(1)} %bitcast.332), kind=kOutput, calls=%fused_computation.2 | convolution fusion | flops 680804352 | bytes 9977856 | tf_op jit(solution)/shard_map/spgk,sgok->spgo/dot_general | solution.py:64
  179.2 1.9 copy.39
  181.3 1.2 copy-done.9
  182.6 1.7 collective-permute-done.8
  184.4 2.1 collective-permute-start.9
  186.4 9.4 %collective-permute-done.9 = bf16[256,768]{1,0:T(8,128)(2,1)S(1)} collective-permute-done((bf16[256,768]{1,0:T(8,128)(2,1)S(1)}, bf16[256,768]{1,0:T(8,128)(2,1)S(1)}, u32[]{:S(2)}, u32[]{:S(2)}) %collective-permute-start.9) | collective-permute-done | bytes 393248 | tf_op jit(solution)/shard_map/ppermute | solution.py:17
  195.8 1.8 collective-permute-start.10
  197.6 13.2 %collective-permute-done.10 = bf16[256,768]{1,0:T(8,128)(2,1)S(1)} collective-permute-done((bf16[256,768]{1,0:T(8,128)(2,1)S(1)}, bf16[256,768]{1,0:T(8,128)(2,1)S(1)}, u32[]{:S(2)}, u32[]{:S(2)}) %collective-permute-start.10) | collective-permute-done | bytes 393248 | tf_op jit(solution)/shard_map/ppermute | solution.py:17
  210.8 4.3 %collective-permute-start.11 = (bf16[256,768]{1,0:T(8,128)(2,1)S(1)}, bf16[256,768]{1,0:T(8,128)(2,1)S(1)}, u32[]{:S(2)}, u32[]{:S(2)}) collective-permute-start(bf16[256,768]{1,0:T(8,128)(2,1)S(1)} %collective-permute-done.10), channel_id=1, source_target_pairs={{0,8},{8,0},{1,9},{9,1},{2,10},{10,2},{3,11},{11,3},{4,12},{12,4},... | collective-permute-start | bytes 1179656 | tf_op jit(solution)/shard_map/ppermute | solution.py:17
  215.1 16.4 %collective-permute-done.11 = bf16[256,768]{1,0:T(8,128)(2,1)S(1)} collective-permute-done((bf16[256,768]{1,0:T(8,128)(2,1)S(1)}, bf16[256,768]{1,0:T(8,128)(2,1)S(1)}, u32[]{:S(2)}, u32[]{:S(2)}) %collective-permute-start.11) | collective-permute-done | bytes 393248 | tf_op jit(solution)/shard_map/ppermute | solution.py:17
  232.0 2.0 fusion.77
  234.0 47.1 %reduce-scatter.5.cloned.1.call-done = f32[48,864]{1,0:T(8,128)} async-done(((f32[768,864]{1,0:T(8,128)}), f32[48,864]{1,0:T(8,128)}) %reduce-scatter.5.cloned.1.call-update) | async-done | bytes 165904 | tf_op jit(solution)/shard_map/reduce_scatter | solution.py:130
  (70 shorter events, 9.8 us)
Async XLA Ops:
  7.2 10.6 %copy-start = (bf16[4,768]{1,0:T(4,128)(2,1)S(1)}, bf16[4,768]{1,0:T(4,128)(2,1)}, u32[]{:S(2)}) copy-start(bf16[4,768]{1,0:T(4,128)(2,1)} %param.6) | copy-start | bytes 18436
  7.2 20.7 %copy-start.10 = (bf16[256,768]{1,0:T(8,128)(2,1)S(1)}, bf16[256,768]{1,0:T(8,128)(2,1)}, u32[]{:S(2)}) copy-start(bf16[256,768]{1,0:T(8,128)(2,1)} %param.9) | copy-start | bytes 1179652
  7.2 106.6 %all-gather.3.cloned.1.call-start = ((), (), s32[]{:S(2)}) async-start(), calls=%async_computation.2 | async-start | bytes 1462272 | tf_op jit(solution)/shard_map/all_gather | solution.py:80
  7.9 112.7 %all-gather.5.cloned.1.call-start = ((), (), s32[]{:S(2)}) async-start(), calls=%async_computation.3 | async-start | bytes 1462272 | tf_op jit(solution)/shard_map/all_gather | solution.py:79
  8.0 1.4 collective-permute-start
  9.4 3.4 %collective-permute-start.1 = (s32[256]{0:T(256)S(1)}, s32[256]{0:T(256)S(1)}, u32[]{:S(2)}, u32[]{:S(2)}) collective-permute-start(s32[256]{0:T(256)S(1)} %collective-permute-done), channel_id=1, source_target_pairs={{0,2},{2,0},{1,3},{3,1},{4,6},{6,4},{5,7},{7,5},{8,10},{10,8},{9,1... | collective-permute-start | bytes 3080 | tf_op jit(solution)/shard_map/ppermute | solution.py:17
  12.7 2.5 collective-permute-start.2
  15.2 3.5 %collective-permute-start.3 = (s32[256]{0:T(256)S(1)}, s32[256]{0:T(256)S(1)}, u32[]{:S(2)}, u32[]{:S(2)}) collective-permute-start(s32[256]{0:T(256)S(1)} %collective-permute-done.2), channel_id=1, source_target_pairs={{0,8},{8,0},{1,9},{9,1},{2,10},{10,2},{3,11},{11,3},{4,12},{12,4},... | collective-permute-start | bytes 3080 | tf_op jit(solution)/shard_map/ppermute | solution.py:17
  18.7 12.7 %copy-start.5 = (bf16[1,256,768]{2,1,0:T(8,128)(2,1)}, bf16[1,256,768]{2,1,0:T(8,128)(2,1)S(1)}, u32[]{:S(2)}) copy-start(bf16[1,256,768]{2,1,0:T(8,128)(2,1)S(1)} %fusion.51) | copy-start | bytes 1179652
  19.1 12.2 %copy-start.7 = (bf16[1,256,768]{2,1,0:T(8,128)(2,1)}, bf16[1,256,768]{2,1,0:T(8,128)(2,1)S(1)}, u32[]{:S(2)}) copy-start(bf16[1,256,768]{2,1,0:T(8,128)(2,1)S(1)} %fusion.52) | copy-start | bytes 1179652
  19.2 8.9 %collective-permute-start.4 = (bf16[2,4,768]{2,1,0:T(4,128)(2,1)S(1)}, bf16[2,4,768]{2,1,0:T(4,128)(2,1)S(1)}, u32[]{:S(2)}, u32[]{:S(2)}) collective-permute-start(bf16[2,4,768]{2,1,0:T(4,128)(2,1)S(1)} %get-tuple-element.9), channel_id=1, source_target_pairs={{0,1},{1,2},{2,3},{3,4},{4,5},{5,6},{6,7},{7,8},{8,9},{9,10},{10,1... | collective-permute-start | bytes 36872 | tf_op jit(solution)/shard_map/ppermute | solution.py:28
  26.0 5.4 %collective-permute-start.5 = (bf16[2,4,768]{2,1,0:T(4,128)(2,1)S(1)}, bf16[2,4,768]{2,1,0:T(4,128)(2,1)S(1)}, u32[]{:S(2)}, u32[]{:S(2)}) collective-permute-start(bf16[2,4,768]{2,1,0:T(4,128)(2,1)S(1)} %get-tuple-element.10), channel_id=1, source_target_pairs={{1,0},{2,1},{3,2},{4,3},{5,4},{6,5},{7,6},{8,7},{9,8},{10,9},{11,1... | collective-permute-start | bytes 36872 | tf_op jit(solution)/shard_map/ppermute | solution.py:30
  27.9 6.9 %collective-permute-start.12 = (bf16[256,768]{1,0:T(8,128)(2,1)S(1)}, bf16[256,768]{1,0:T(8,128)(2,1)S(1)}, u32[]{:S(2)}, u32[]{:S(2)}) collective-permute-start(bf16[256,768]{1,0:T(8,128)(2,1)S(1)} %copy-done.10), channel_id=1, source_target_pairs={{0,1},{1,0},{2,3},{3,2},{4,5},{5,4},{6,7},{7,6},{8,9},{9,8},{10,11... | collective-permute-start | bytes 1179656 | tf_op jit(solution)/shard_map/ppermute | solution.py:17
  28.0 206.0 %reduce-scatter.3.cloned.1.call-start = ((), (), s32[]{:S(2)}) async-start(), calls=%async_computation.4 | async-start | bytes 2924544 | tf_op jit(solution)/shard_map/reduce_scatter | solution.py:129
  34.8 13.3 %collective-permute-start.13 = (bf16[256,768]{1,0:T(8,128)(2,1)S(1)}, bf16[256,768]{1,0:T(8,128)(2,1)S(1)}, u32[]{:S(2)}, u32[]{:S(2)}) collective-permute-start(bf16[256,768]{1,0:T(8,128)(2,1)S(1)} %collective-permute-done.12), channel_id=1, source_target_pairs={{0,2},{2,0},{1,3},{3,1},{4,6},{6,4},{5,7},{7,5},{8,10},{10,8},{9,1... | collective-permute-start | bytes 1179656 | tf_op jit(solution)/shard_map/ppermute | solution.py:17
  48.1 12.7 %collective-permute-start.14 = (bf16[256,768]{1,0:T(8,128)(2,1)S(1)}, bf16[256,768]{1,0:T(8,128)(2,1)S(1)}, u32[]{:S(2)}, u32[]{:S(2)}) collective-permute-start(bf16[256,768]{1,0:T(8,128)(2,1)S(1)} %collective-permute-done.13), channel_id=1, source_target_pairs={{0,4},{4,0},{1,5},{5,1},{2,6},{6,2},{3,7},{7,3},{8,12},{12,8},{9,1... | collective-permute-start | bytes 1179656 | tf_op jit(solution)/shard_map/ppermute | solution.py:17
  60.8 22.5 %collective-permute-start.15 = (bf16[256,768]{1,0:T(8,128)(2,1)S(1)}, bf16[256,768]{1,0:T(8,128)(2,1)S(1)}, u32[]{:S(2)}, u32[]{:S(2)}) collective-permute-start(bf16[256,768]{1,0:T(8,128)(2,1)S(1)} %collective-permute-done.14), channel_id=1, source_target_pairs={{0,8},{8,0},{1,9},{9,1},{2,10},{10,2},{3,11},{11,3},{4,12},{12,4},... | collective-permute-start | bytes 1179656 | tf_op jit(solution)/shard_map/ppermute | solution.py:17
  83.7 18.2 %copy-start.3 = (bf16[256,768]{1,0:T(8,128)(2,1)}, bf16[256,768]{1,0:T(8,128)(2,1)S(1)}, u32[]{:S(2)}) copy-start(bf16[256,768]{1,0:T(8,128)(2,1)S(1)} %rev.16) | copy-start | bytes 1179652
  83.8 18.1 %collective-permute-start.16 = (bf16[2,4,768]{2,1,0:T(4,128)(2,1)S(1)}, bf16[2,4,768]{2,1,0:T(4,128)(2,1)S(1)}, u32[]{:S(2)}, u32[]{:S(2)}) collective-permute-start(bf16[2,4,768]{2,1,0:T(4,128)(2,1)S(1)} %get-tuple-element.5), channel_id=1, source_target_pairs={{0,1},{1,2},{2,3},{3,4},{4,5},{5,6},{6,7},{7,8},{8,9},{9,10},{10,1... | collective-permute-start | bytes 36872 | tf_op jit(solution)/shard_map/ppermute | solution.py:28
  86.7 15.1 %collective-permute-start.17 = (bf16[2,4,768]{2,1,0:T(4,128)(2,1)S(1)}, bf16[2,4,768]{2,1,0:T(4,128)(2,1)S(1)}, u32[]{:S(2)}, u32[]{:S(2)}) collective-permute-start(bf16[2,4,768]{2,1,0:T(4,128)(2,1)S(1)} %get-tuple-element.6), channel_id=1, source_target_pairs={{1,0},{2,1},{3,2},{4,3},{5,4},{6,5},{7,6},{8,7},{9,8},{10,9},{11,1... | collective-permute-start | bytes 36872 | tf_op jit(solution)/shard_map/ppermute | solution.py:30
  146.3 134.8 %reduce-scatter.5.cloned.1.call-start = ((), (), s32[]{:S(2)}) async-start(), calls=%async_computation.5 | async-start | bytes 2924544 | tf_op jit(solution)/shard_map/reduce_scatter | solution.py:130
  150.8 6.2 %copy-start.11 = (bf16[256,768]{1,0:T(8,128)(2,1)S(1)}, bf16[256,768]{1,0:T(8,128)(2,1)}, u32[]{:S(2)}) copy-start(bf16[256,768]{1,0:T(8,128)(2,1)} %param.9) | copy-start | bytes 1179652
  150.8 6.4 %copy-start.4 = (bf16[256,768]{1,0:T(8,128)(2,1)S(1)}, bf16[256,768]{1,0:T(8,128)(2,1)}, u32[]{:S(2)}) copy-start(bf16[256,768]{1,0:T(8,128)(2,1)} %copy-done.3) | copy-start | bytes 1179652
  151.0 8.5 %collective-permute-start.6 = (bf16[2,4,768]{1,2,0:T(8,128)(2,1)S(1)}, bf16[2,4,768]{1,2,0:T(8,128)(2,1)S(1)}, u32[]{:S(2)}, u32[]{:S(2)}) collective-permute-start(bf16[2,4,768]{1,2,0:T(8,128)(2,1)S(1)} %get-tuple-element.7), channel_id=1, source_target_pairs={{0,1},{1,2},{2,3},{3,4},{4,5},{5,6},{6,7},{7,8},{8,9},{9,10},{10,1... | collective-permute-start | bytes 36872 | tf_op jit(solution)/shard_map/ppermute | solution.py:28
  154.8 9.1 %collective-permute-start.7 = (bf16[2,4,768]{1,2,0:T(8,128)(2,1)S(1)}, bf16[2,4,768]{1,2,0:T(8,128)(2,1)S(1)}, u32[]{:S(2)}, u32[]{:S(2)}) collective-permute-start(bf16[2,4,768]{1,2,0:T(8,128)(2,1)S(1)} %get-tuple-element.8), channel_id=1, source_target_pairs={{1,0},{2,1},{3,2},{4,3},{5,4},{6,5},{7,6},{8,7},{9,8},{10,9},{11,1... | collective-permute-start | bytes 36872 | tf_op jit(solution)/shard_map/ppermute | solution.py:30
  167.5 2.9 copy-start.2
  172.2 1.3 copy-start.12
  179.2 2.0 copy-start.6
  179.2 2.0 copy-start.8
  181.2 99.9 %copy-start.1 = (bf16[4,768]{1,0:T(4,128)(2,1)S(1)}, bf16[4,768]{1,0:T(4,128)(2,1)}, u32[]{:S(2)}) copy-start(bf16[4,768]{1,0:T(4,128)(2,1)} %param.6) | copy-start | bytes 18436
  181.3 1.2 copy-start.9
  182.6 1.8 collective-permute-start.8
  184.4 11.4 %collective-permute-start.9 = (bf16[256,768]{1,0:T(8,128)(2,1)S(1)}, bf16[256,768]{1,0:T(8,128)(2,1)S(1)}, u32[]{:S(2)}, u32[]{:S(2)}) collective-permute-start(bf16[256,768]{1,0:T(8,128)(2,1)S(1)} %collective-permute-done.8), channel_id=1, source_target_pairs={{0,2},{2,0},{1,3},{3,1},{4,6},{6,4},{5,7},{7,5},{8,10},{10,8},{9,1... | collective-permute-start | bytes 1179656 | tf_op jit(solution)/shard_map/ppermute | solution.py:17
  195.8 15.0 %collective-permute-start.10 = (bf16[256,768]{1,0:T(8,128)(2,1)S(1)}, bf16[256,768]{1,0:T(8,128)(2,1)S(1)}, u32[]{:S(2)}, u32[]{:S(2)}) collective-permute-start(bf16[256,768]{1,0:T(8,128)(2,1)S(1)} %collective-permute-done.9), channel_id=1, source_target_pairs={{0,4},{4,0},{1,5},{5,1},{2,6},{6,2},{3,7},{7,3},{8,12},{12,8},{9,1... | collective-permute-start | bytes 1179656 | tf_op jit(solution)/shard_map/ppermute | solution.py:17
  210.8 20.7 %collective-permute-start.11 = (bf16[256,768]{1,0:T(8,128)(2,1)S(1)}, bf16[256,768]{1,0:T(8,128)(2,1)S(1)}, u32[]{:S(2)}, u32[]{:S(2)}) collective-permute-start(bf16[256,768]{1,0:T(8,128)(2,1)S(1)} %collective-permute-done.10), channel_id=1, source_target_pairs={{0,8},{8,0},{1,9},{9,1},{2,10},{10,2},{3,11},{11,3},{4,12},{12,4},... | collective-permute-start | bytes 1179656 | tf_op jit(solution)/shard_map/ppermute | solution.py:17
Sparse Core Ops, SparseCore 0:
  10.2 44.2 all-gather.2
  56.6 47.0 all-gather.4
  146.4 66.7 reduce-scatter.2
  217.4 63.6 reduce-scatter.4
where the time goes:
time: 290 us; the launch traced here: 288 us
  waiting for transfers between devices  137 us (47%)
  local copies, waits for them, and re-layouts  51 us (18%)
  starting transfers between devices  40.7 us (14%)
  matrix products  30.2 us (10%)
  between operations  14.2 us (5%)
  other arithmetic  14.1 us (5%)
    ppermute x12, waiting for transfers between devices, from_partner(): return lax.ppermute(block, axis, route)  79.7 us
    reduce_scatter x1, waiting for transfers between devices, per_device(): lax.psum_scatter(second_local.reshape(channels, -1), 'seq', scatter_dimen...  47.1 us
    unnamed x51, local copies, waits for them, and re-layouts  24.2 us
    ppermute x12, starting transfers between devices, from_partner(): return lax.ppermute(block, axis, route)  21 us
    dot_general x2, matrix products, correlate(): jnp.einsum('spgo,spgk->sgok', grad_groups, columns, preferred_element_typ...  16.7 us
    another operation x4, local copies, waits for them, and re-layouts, unfold(): jnp.stack([pieces[:, tap_index:tap_index + out_rows] for tap_index in ran...  14.8 us
    ppermute x3, starting transfers between devices, extended_2(): lax.ppermute(tail, axis, [(i, (i + 1) % count) for i in range(ends)])  13.6 us
    dot_general x2, matrix products, conv_cols(): jnp.einsum('spgk,sgok->spgo', columns, kernels, preferred_element_type=jn...  12.3 us
  transfers between devices with their start and end apart: 22, of which 14 were waited for; matrix products, arithmetic and copies ran while one was open for 23% of the time, Pallas kernels for 0%

commit v1 on v0

v1 whole, which is shorter than its diff:
```python
import functools
import math

import jax
import jax.numpy as jnp
from jax import lax
from jax.experimental import pallas as pl
from jax.experimental.pallas import tpu as pltpu
from jax.sharding import PartitionSpec as P

GROUPS = 8
TAPS = 9
HALF = TAPS // 2
LANES = 128
HIGH = 128
MESH = pl.DeviceIdType.MESH
F32 = jnp.float32
BF16 = jnp.bfloat16


def lane_contract(left, right):
    return lax.dot_general(left, right, (((1,), (1,)), ((), ())), preferred_element_type=F32)


def split_halves(values, axis):
    high = values.astype(BF16).astype(F32)
    column = lax.broadcasted_iota(jnp.int32, values.shape, axis) & 7
    return jnp.where(column < 4, high, values - high).astype(BF16)


def block_kernel(
    count, members, gathered, step,
    codes_ref, diag_ref, skip_ref, first_ref, second_ref, cot_ref,
    comb_ref, first_out, second_out,
    cot_t, codes_in, codes_left, codes_right, cot_in, cot_left, cot_right,
    first_all, second_all, onehot, hid, slope, unf_f, unf_r, cot_unf, adj,
    s_acc, comb_send, comb_in, s_send, s_in, g_send, g_in,
    send_sems, recv_sems,
):
    me = lax.axis_index("seq")
    group = me // members
    member = me % members
    chunk_of = me // GROUPS
    band_of = me % GROUPS
    band = cot_ref.shape[0]
    chunk = band * GROUPS
    width = chunk + LANES
    cg = cot_t.shape[0] // GROUPS
    rows = cg // members
    started = []

    def push(src, dst, kind, recv, target):
        remote = pltpu.make_async_remote_copy(
            src_ref=src, dst_ref=dst, send_sem=send_sems.at[kind], recv_sem=recv_sems.at[recv],
            device_id={"seq": target}, device_id_type=MESH,
        )

        @pl.when(target != me)
        def _():
            remote.start()

        @pl.when(target == me)
        def _():
            pltpu.make_async_copy(src, dst, recv_sems.at[recv]).start()

        started.append((remote, target, None))

    def arrived(ref, recv):
        pltpu.make_async_copy(ref, ref, recv_sems.at[recv]).wait()

    def push_edges(src_of, left_dst, right_dst, kind, recv_left, recv_right):
        for low, dst, recv, here, there in (
            (True, right_dst, recv_right, (band_of == 0) & (chunk_of > 0), chunk_of - 1),
            (False, left_dst, recv_left, (band_of == GROUPS - 1) & (chunk_of < members - 1), chunk_of + 1),
        ):
            for g in range(GROUPS):
                src = src_of(g, low)
                target = g * members + there
                remote = pltpu.make_async_remote_copy(
                    src_ref=src, dst_ref=dst, send_sem=send_sems.at[kind], recv_sem=recv_sems.at[recv],
                    device_id={"seq": target}, device_id_type=MESH,
                )

                @pl.when(here & (target != me))
                def _():
                    remote.start()

                @pl.when(here & (target == me))
                def _():
                    pltpu.make_async_copy(src, dst, recv_sems.at[recv]).start()

                started.append((remote, target, here))

    def edges_arrived(left, right, recv_left, recv_right):
        @pl.when(member > 0)
        def _():
            arrived(left, recv_left)

        @pl.when(member < members - 1)
        def _():
            arrived(right, recv_right)

    barrier = pltpu.get_barrier_semaphore()
    for k in range(1, count):
        pl.semaphore_signal(barrier, inc=1, device_id={"seq": (me + k) % count}, device_id_type=MESH)
    cot_t[...] = jnp.transpose(cot_ref[...])
    hid[...] = jnp.zeros_like(hid)
    pl.semaphore_wait(barrier, count - 1)

    place = pl.ds(pl.multiple_of(band_of * band, LANES), band)
    for g in range(GROUPS):
        push(codes_ref, codes_in.at[:, place], 0, 0, g * members + chunk_of)
    push_edges(
        lambda g, low: codes_ref.at[:, pl.ds(0 if low else band - LANES, LANES)],
        codes_left, codes_right, 1, 1, 2,
    )
    if gathered:
        first = first_ref[...]
        second = second_ref[...]
    else:
        for k in range(members):
            push(first_ref, first_all.at[member], 2, 3, group * members + k)
        for k in range(members):
            push(second_ref, second_all.at[member], 3, 4, group * members + k)
    for g in range(GROUPS):
        push(cot_t.at[pl.ds(cg * g, cg)], cot_in.at[:, place], 4, 5, g * members + chunk_of)
    push_edges(
        lambda g, low: cot_t.at[pl.ds(cg * g, cg), pl.ds(0 if low else band - LANES, LANES)],
        cot_left, cot_right, 5, 6, 7,
    )

    has_right = (member < members - 1).astype(jnp.int32)
    has_left = (member > 0).astype(jnp.int32)

    def edge_mask(height):
        lane = lax.broadcasted_iota(jnp.int32, (height, LANES), 1)
        return lane < LANES // 2, jnp.where(lane < LANES // 2, has_right, has_left) > 0

    arrived(codes_in, 0)
    edges_arrived(codes_left, codes_right, 1, 2)
    on_right, real = edge_mask(8)
    edge = jnp.where(real, jnp.where(on_right, codes_right[...], codes_left[...]), 4)
    codes = jnp.concatenate([codes_in[...], edge], axis=1)
    want = lax.broadcasted_iota(jnp.int32, (8, width), 0) & 3
    onehot[...] = jnp.concatenate(
        [
            jnp.where(pltpu.roll(codes, (HALF - u) % width, 1) == want, 1.0, 0.0)
            for u in range(TAPS)
        ],
        axis=0,
    ).astype(BF16)

    if not gathered:
        arrived(first_all, 3)
        first = first_all[...].reshape(cg, TAPS * cg)
    mix = jnp.concatenate(
        [split_halves(lane_contract(first, diag_ref[s]), 1) for s in range(2)], axis=0
    )

    def activate(cols):
        pre = jnp.dot(mix, onehot[:, cols], preferred_element_type=F32)
        cdf = 0.5 + 0.5 * lax.erf(pre * math.sqrt(0.5))
        return pre * cdf, cdf + pre * jnp.exp(-0.5 * pre * pre) * (1.0 / math.sqrt(2.0 * math.pi))

    @pl.loop(0, chunk // 256)
    def _(i):
        cols = pl.ds(pl.multiple_of(i * 256, 256), 256)
        hidden, grad = activate(cols)
        hidden = hidden.astype(BF16)
        hid[0:cg, cols] = hidden[:cg]
        hid[HIGH : HIGH + cg, cols] = hidden[cg:]
        slope[:, cols] = grad

    hidden, _ = activate(pl.ds(chunk, LANES))
    _, real = edge_mask(2 * cg)
    hidden = jnp.where(real, hidden, 0.0).astype(BF16)
    hid[0:cg, chunk:] = hidden[:cg]
    hid[HIGH : HIGH + cg, chunk:] = hidden[cg:]

    for t in range(TAPS):
        unf_f[cg * t : cg * (t + 1), :] = pltpu.roll(hid[0:cg, :], (HALF - t) % width, 1)[:, :chunk]
        unf_r[cg * t : cg * (t + 1), :] = pltpu.roll(
            hid[HIGH : HIGH + cg, :], (t - HALF) % width, 1
        )[:, :chunk]

    if not gathered:
        arrived(second_all, 4)
        second = second_all[...].reshape(cg, TAPS * cg)

    @pl.loop(0, chunk // step)
    def _(i):
        cols = pl.ds(pl.multiple_of(i * step, step), step)
        out_f = jnp.dot(second, unf_f[:, cols], preferred_element_type=F32)
        out_f += jnp.dot(skip_ref[0], onehot[:, cols], preferred_element_type=F32)
        out_r = jnp.dot(second, unf_r[:, cols], preferred_element_type=F32)
        out_r += jnp.dot(skip_ref[1], onehot[:, cols], preferred_element_type=F32)
        comb_send[:, cols] = (out_f + out_r.astype(BF16).astype(F32)).astype(BF16)

    for j in range(GROUPS):
        push(comb_send.at[:, pl.ds(j * band, band)], comb_in.at[group], 6, 8, member * GROUPS + j)

    arrived(cot_in, 5)
    edges_arrived(cot_left, cot_right, 6, 7)
    on_right, real = edge_mask(cg)
    edge = jnp.where(
        real, jnp.where(on_right, cot_right[...].astype(F32), cot_left[...].astype(F32)), 0.0
    ).astype(BF16)
    cot = jnp.concatenate([cot_in[...], edge], axis=1)
    for t in range(TAPS):
        cot_unf[cg * t : cg * (t + 1), :] = pltpu.roll(cot, (HALF - t) % width, 1)[:, :chunk]

    s_acc[...] = jnp.zeros_like(s_acc)

    @pl.loop(0, chunk // step)
    def _(i):
        cols = pl.ds(pl.multiple_of(i * step, step), step)
        s_acc[...] += lane_contract(cot_unf[:, cols], hid[:, cols])

    for t in range(TAPS):
        block = (
            s_acc[cg * (TAPS - 1 - t) : cg * (TAPS - t), 0:cg]
            + s_acc[cg * t : cg * (t + 1), HIGH : HIGH + cg]
        )
        if gathered:
            second_out[t] = block
        else:
            for k in range(members):
                s_send[k, t] = block[rows * k : rows * (k + 1)]
    if not gathered:
        for k in range(members):
            push(s_send.at[k], s_in.at[member], 7, 9, group * members + k)

    turned = jnp.transpose(second)
    for u in range(TAPS):
        v = TAPS - 1 - u
        adj[u, 0:cg] = turned[cg * v : cg * (v + 1)]
        adj[u, cg:] = turned[cg * u : cg * (u + 1)]

    def backward(i, total):
        cols = pl.ds(pl.multiple_of(i * step, step), step)
        grad = jnp.dot(adj[0], cot_unf[0:cg, cols], preferred_element_type=F32)
        for u in range(1, TAPS):
            grad += jnp.dot(adj[u], cot_unf[cg * u : cg * (u + 1), cols], preferred_element_type=F32)
        pre_grad = (grad * slope[:, cols]).astype(BF16)
        return total + lane_contract(pre_grad, onehot[:, cols])

    terms = lax.fori_loop(0, chunk // step, backward, jnp.zeros((2 * cg, 8 * TAPS), F32))
    if gathered:
        first_out[0] = terms[:cg]
        first_out[1] = terms[cg:]
    else:
        for k in range(members):
            for s in range(2):
                g_send[k, s] = terms[s * cg + rows * k : s * cg + rows * (k + 1)]
        for k in range(members):
            push(g_send.at[k], g_in.at[member], 8, 10, group * members + k)

    arrived(comb_in, 8)
    comb_ref[...] = jnp.transpose(comb_in[...].reshape(GROUPS * cg, band))
    if not gathered:
        arrived(s_in, 9)
        second_out[...] = jnp.sum(s_in[...], axis=0)
        arrived(g_in, 10)
        summed = jnp.sum(g_in[...], axis=0)
        first_out[...] = jnp.dot(
            split_halves(summed[0], 1), diag_ref[0], preferred_element_type=F32
        ) + jnp.dot(split_halves(summed[1], 1), diag_ref[1], preferred_element_type=F32)

    for remote, target, here in started:
        @pl.when((target != me) if here is None else (here & (target != me)))
        def _():
            remote.wait_send()


def per_device(bases, base_table, first_kernel, second_kernel, cotangent):
    band, channels = cotangent.shape
    cg = channels // GROUPS
    count = lax.axis_size("seq")
    members = count // GROUPS
    rows = first_kernel.shape[0]
    chunk = band * GROUPS
    width = chunk + LANES
    step = math.gcd(chunk, 512)
    me = lax.axis_index("seq")
    gathered = rows % 16 != 0

    table = lax.dynamic_slice_in_dim(base_table, (me // members) * cg, cg, axis=1)
    columns = 8 * TAPS
    offset = jnp.arange(columns) // 8
    high = jnp.arange(columns) % 8 < 4
    tap = jnp.arange(TAPS * cg) // cg
    zero = jnp.zeros((), BF16)
    diag, skip = [], []
    for s in range(2):
        strand = table if s == 0 else table[::-1]
        wanted = offset if s == 0 else TAPS - 1 - offset
        diag.append(jnp.where(wanted[:, None] == tap[None, :], jnp.tile(strand, (2 * TAPS, TAPS)), zero))
        chosen = ((offset == HALF) & high)[None, :]
        skip.append(jnp.where(chosen, jnp.tile(strand.T, (1, 2 * TAPS)), zero))
    diag, skip = jnp.stack(diag), jnp.stack(skip)
    codes = jnp.broadcast_to(bases[None, :], (8, band))

    if gathered:
        same = [[g * members + k for k in range(members)] for g in range(GROUPS)]
        first_kernel = lax.all_gather(first_kernel, "seq", axis=0, tiled=True, axis_index_groups=same)
        second_kernel = lax.all_gather(second_kernel, "seq", axis=0, tiled=True, axis_index_groups=same)
        outs = ((2, cg, columns), (TAPS, cg, cg))
        lot, lot_rows = 1, 16
    else:
        outs = ((rows, TAPS * cg), (TAPS, rows, cg))
        lot, lot_rows = members, rows

    vmem = pltpu.VMEM
    combined, first_grad, second_grad = pl.pallas_call(
        functools.partial(block_kernel, count, members, gathered, step),
        out_shape=(
            jax.ShapeDtypeStruct((band, channels), BF16),
            jax.ShapeDtypeStruct(outs[0], F32),
            jax.ShapeDtypeStruct(outs[1], F32),
        ),
        in_specs=[pl.BlockSpec(memory_space=vmem)] * 6,
        out_specs=[pl.BlockSpec(memory_space=vmem)] * 3,
        scratch_shapes=[
            vmem((channels, band), BF16),
            vmem((8, chunk), jnp.int32),
            vmem((8, LANES), jnp.int32),
            vmem((8, LANES), jnp.int32),
            vmem((cg, chunk), BF16),
            vmem((cg, LANES), BF16),
            vmem((cg, LANES), BF16),
            vmem((lot, lot_rows, TAPS * cg), BF16),
            vmem((lot, lot_rows, TAPS * cg), BF16),
            vmem((columns, width), BF16),
            vmem((2 * HIGH, width), BF16),
            vmem((2 * cg, chunk), F32),
            vmem((TAPS * cg, chunk), BF16),
            vmem((TAPS * cg, chunk), BF16),
            vmem((TAPS * cg, chunk), BF16),
            vmem((TAPS, 2 * cg, cg), BF16),
            vmem((TAPS * cg, 2 * HIGH), F32),
            vmem((cg, chunk), BF16),
            vmem((GROUPS, cg, band), BF16),
            vmem((lot, TAPS, lot_rows, cg), F32),
            vmem((lot, TAPS, lot_rows, cg), F32),
            vmem((lot, 2, lot_rows, columns), F32),
            vmem((lot, 2, lot_rows, columns), F32),
            pltpu.SemaphoreType.DMA((9,)),
            pltpu.SemaphoreType.DMA((11,)),
        ],
        compiler_params=pltpu.CompilerParams(
            collective_id=0, has_side_effects=True, vmem_limit_bytes=56 * 1024 * 1024
        ),
    )(codes, diag, skip, first_kernel, second_kernel, cotangent)

    if gathered:
        first_local = jnp.zeros((cg, TAPS * cg), F32)
        for s in range(2):
            first_local += jnp.einsum(
                "oc,ck->ok",
                jnp.where(high[None, :], first_grad[s], 0.0),
                diag[s].astype(F32),
                precision=lax.Precision.HIGHEST,
            )
        second_local = jnp.transpose(second_grad, (1, 0, 2)).reshape(cg, TAPS * cg)
        scatter = functools.partial(
            lax.psum_scatter, axis_name="seq", scatter_dimension=0, tiled=True, axis_index_groups=same
        )
        return combined, scatter(first_local), scatter(second_local)
    return combined, first_grad, jnp.transpose(second_grad, (1, 0, 2)).reshape(rows, TAPS * cg)


def solution(mesh):
    return jax.shard_map(
        per_device,
        mesh=mesh,
        in_specs=(
            P(("groups", "seq")),
            P(),
            P("seq", None),
            P("seq", None),
            P(("groups", "seq"), None),
        ),
        out_specs=(
            P(("groups", "seq"), None),
            P(("groups", "seq"), None),
            P(("groups", "seq"), None),
        ),
        check_vma=False,
    )
```

time: 290 us -> 38.5 us (0.13)
  waiting for transfers between devices: 137 us -> 0 us
  local copies, waits for them, and re-layouts: 51 us -> 6.58 us
  starting transfers between devices: 40.7 us -> 0 us
  matrix products: 30.2 us -> 0 us
  Pallas kernels: 0 us -> 29.3 us
  between operations: 14.2 us -> 0.76 us
  other arithmetic: 14.1 us -> 1.54 us
    ppermute x18 -> x0, waiting for transfers between devices: 89.6 us -> none  [the longest x12 79.7 us: from_partner(): return lax.ppermute(block, axis, route)]
    reduce_scatter x2 -> x0, waiting for transfers between devices: 47.1 us -> none  [the longest x1 47.1 us: per_device(): lax.psum_scatter(second_local.reshape(channels, -1), 'seq', scatter_dimen...]
    ppermute x18 -> x0, starting transfers between devices: 40.6 us -> none  [the longest x12 21 us: from_partner(): return lax.ppermute(block, axis, route)]
    dot_general x6 -> x0, matrix products: 30.2 us -> none  [the longest x2 16.7 us: correlate(): jnp.einsum('spgo,spgk->sgok', grad_groups, columns, preferred_element_typ...]
    pallas_call x0 -> x1, Pallas kernels: none -> 29.3 us  [per_device(): pl.pallas_call(functools.partial(block_kernel, count, members, gathered,...]
    unnamed x51 -> x10, local copies, waits for them, and re-layouts: 24.2 us -> 3.25 us
    another operation x6 -> x8, local copies, waits for them, and re-layouts: 18.3 us -> 0.74 us  [the longest x4 0.52 us: per_device(): jnp.tile(strand, (2 * TAPS, TAPS))]
    add x3 -> x0, other arithmetic: 6.48 us -> none  [the longest x1 4.48 us: per_device(): first_local = first_terms[0] + first_terms[1]]
  transfers between devices with their start and end apart: 22 -> 0, of which waited for: 14 -> 0; matrix products, arithmetic and copies ran while one was open for 23% -> 0% of each run, Pallas kernels for 0% -> 0%
where the time goes in v1:
time: 38.5 us; the launch traced here: 38.2 us
  Pallas kernels  29.3 us (76%)
  local copies, waits for them, and re-layouts  6.58 us (17%)
  other arithmetic  1.54 us (4%)
  between operations  0.76 us (2%)
    pallas_call x1, Pallas kernels, per_device(): pl.pallas_call(functools.partial(block_kernel, count, members, gathered,...  29.3 us
    unnamed x10, local copies, waits for them, and re-layouts  3.25 us
    another operation x2, other arithmetic, per_device(): diag, skip = (jnp.stack(diag), jnp.stack(skip))  1.37 us
    transpose x1, local copies, waits for them, and re-layouts, per_device(): jnp.transpose(second_grad, (1, 0, 2)).reshape(rows, TAPS * cg)  1.02 us
    reshape x1, local copies, waits for them, and re-layouts, per_device(): jnp.transpose(second_grad, (1, 0, 2)).reshape(rows, TAPS * cg)  0.79 us

profile of v1, /device:TPU:1, one launch (start us, length us, event | category | flops | bytes accessed | tf_op | source)
XLA Modules:
  0.0 38.2 jit_solution(637565460795182773)
XLA Ops:
  0.6 0.0 copy-start
  0.7 0.7 %copy-done = bf16[4,768]{1,0:T(4,128)(2,1)S(1)} copy-done((bf16[4,768]{1,0:T(4,128)(2,1)S(1)}, bf16[4,768]{1,0:T(4,128)(2,1)}, u32[]{:S(2)}) %copy-start) | copy-done | bytes 6168
  1.3 0.1 constant_dynamic-slice_fusion
  1.4 0.1 fusion.3
  1.5 0.0 copy-start.3
  1.5 0.7 %copy-done.3 = s32[256]{0:T(256)S(1)} copy-done((s32[256]{0:T(256)S(1)}, s32[256]{0:T(256)}, u32[]{:S(2)}) %copy-start.3) | copy-done | bytes 1048
  2.2 0.6 %broadcast_in_dim.35.codes_ref = s32[8,256]{1,0:T(8,128)} broadcast(s32[256]{0:T(256)S(1)} %copy-done.3), dimensions={1} | broadcast | bytes 9216 | tf_op jit(solution)/shard_map/broadcast_in_dim | solution.py:301
  2.8 0.1 copy.10
  2.9 0.1 copy.11
  3.0 0.6 %pad_maximum_fusion.1.skip_ref = bf16[2,96,72]{2,1,0:T(8,128)(2,1)} fusion(bf16[1,96,72]{2,1,0:T(8,128)(2,1)S(1)} %get-tuple-element.12, bf16[1,96,72]{2,1,0:T(8,128)(2,1)S(1)} %get-tuple-element.11), kind=kLoop, calls=%fused_computation.3 | loop fusion | flops 13824 | bytes 55296 | tf_op jit(solution)/shard_map/stack | solution.py:300
  3.7 0.1 tile.16
  3.7 0.2 tile.17
  4.0 0.1 tile.18
  4.0 0.2 tile.19
  4.2 0.1 compare_select_fusion.1
  4.4 0.7 %pad_maximum_fusion.diag_ref = bf16[2,72,864]{2,1,0:T(8,128)(2,1)} fusion(bf16[1,72,864]{2,1,0:T(8,128)(2,1)S(1)} %get-tuple-element.10, bf16[1,72,864]{2,1,0:T(8,128)(2,1)S(1)} %get-tuple-element.9), kind=kLoop, calls=%fused_computation | loop fusion | flops 124416 | bytes 497664 | tf_op jit(solution)/shard_map/stack | solution.py:300
  5.1 29.3 %shard_map.76 = (bf16[256,768]{1,0:T(8,128)(2,1)}, f32[48,864]{1,0:T(8,128)}, f32[9,48,96]{2,1,0:T(8,128)}) custom-call(s32[8,256]{1,0:T(8,128)} %broadcast_in_dim.35.codes_ref, bf16[2,72,864]{2,1,0:T(8,128)(2,1)} %pad_maximum_fusion.diag_ref, bf16[2,96,72]{2,1,0:T(8,128)(2,1)} %pad_maximum_fusion.1.skip_ref, bf16[48,864]{1,0:T(8,128)(2,1)} %first_ref.1, ...), custom_call_target="tpu_custom_call" | custom-call | tf_op jit(solution)/shard_map/pallas_call | solution.py:314
  34.5 1.0 %copy.12 = f32[48,9,96]{2,1,0:T(8,128)S(1)} copy(f32[48,9,96]{2,0,1:T(8,128)} %bitcast.6) | data formatting | bytes 331776 | tf_op jit(solution)/shard_map/transpose | solution.py:369
  35.5 0.0 copy-start.1
  35.5 0.8 %reshape.246 = f32[48,864]{1,0:T(8,128)} reshape(f32[48,9,96]{2,1,0:T(8,128)S(1)} %copy.12) | data formatting | bytes 331776 | tf_op jit(solution)/shard_map/reshape | solution.py:369
  36.3 0.2 copy-done.1
  36.5 0.0 copy-start.2
  36.5 0.7 %copy.15 = bf16[256,768]{1,0:T(8,128)(2,1)} copy(bf16[256,768]{1,0:T(8,128)(2,1)S(1)} %copy-done.1) | data formatting | bytes 786432
  37.2 0.3 copy-done.2
  37.5 0.7 %copy.16 = f32[48,864]{1,0:T(8,128)} copy(f32[48,864]{1,0:T(8,128)S(1)} %copy-done.2) | data formatting | bytes 331776
  (7 shorter events, 0.1 us)
Async XLA Ops:
  0.6 0.7 %copy-start = (bf16[4,768]{1,0:T(4,128)(2,1)S(1)}, bf16[4,768]{1,0:T(4,128)(2,1)}, u32[]{:S(2)}) copy-start(bf16[4,768]{1,0:T(4,128)(2,1)} %param.6) | copy-start | bytes 18436
  1.5 0.7 %copy-start.3 = (s32[256]{0:T(256)S(1)}, s32[256]{0:T(256)}, u32[]{:S(2)}) copy-start(s32[256]{0:T(256)} %param.5) | copy-start | bytes 3076
  35.5 1.0 %copy-start.1 = (bf16[256,768]{1,0:T(8,128)(2,1)S(1)}, bf16[256,768]{1,0:T(8,128)(2,1)}, u32[]{:S(2)}) copy-start(bf16[256,768]{1,0:T(8,128)(2,1)} %get-tuple-element.18) | copy-start | bytes 1179652
  36.5 1.1 %copy-start.2 = (f32[48,864]{1,0:T(8,128)S(1)}, f32[48,864]{1,0:T(8,128)}, u32[]{:S(2)}) copy-start(f32[48,864]{1,0:T(8,128)} %get-tuple-element.19) | copy-start | bytes 497668

commit v2 on v1

--- a/solution.py
+++ b/solution.py
@@ -30,12 +30,12 @@
 
 def block_kernel(
     count, members, gathered, step,
-    codes_ref, diag_ref, skip_ref, first_ref, second_ref, cot_ref,
-    comb_ref, first_out, second_out,
-    cot_t, codes_in, codes_left, codes_right, cot_in, cot_left, cot_right,
+    bases_ref, table_ref, first_ref, second_ref, cot_ref,
+    comb_in, first_out, second_out, diag_out,
+    diag_ref, skip_ref, edges, codes_ref, cot_t, codes_in, codes_left, codes_right, cot_in, cot_left, cot_right,
     first_all, second_all, onehot, hid, slope, unf_f, unf_r, cot_unf, adj,
-    s_acc, comb_send, comb_in, s_send, s_in, g_send, g_in,
-    send_sems, recv_sems,
+    s_acc, comb_send, s_send, g_send,
+    send_sems, recv_sems, diag_sem,
 ):
     me = lax.axis_index("seq")
     group = me // members
@@ -46,14 +46,21 @@
     chunk = band * GROUPS
     width = chunk + LANES
     cg = cot_t.shape[0] // GROUPS
-    rows = cg // members
+    s_rows = cg if gathered else cg // members
     started = []
 
-    def push(src, dst, kind, recv, target):
+    def keep_for_send(src, dst, kind, recv, target):
         remote = pltpu.make_async_remote_copy(
             src_ref=src, dst_ref=dst, send_sem=send_sems.at[kind], recv_sem=recv_sems.at[recv],
             device_id={"seq": target}, device_id_type=MESH,
         )
+        started.append((remote, target, None))
+        return remote
+
+    def push(src, dst, kind, recv, target, keep=True):
+        remote = keep_for_send(src, dst, kind, recv, target)
+        if not keep:
+            started.pop()
 
         @pl.when(target != me)
         def _():
@@ -62,8 +69,6 @@
         @pl.when(target == me)
         def _():
             pltpu.make_async_copy(src, dst, recv_sems.at[recv]).start()
-
-        started.append((remote, target, None))
 
     def arrived(ref, recv):
         pltpu.make_async_copy(ref, ref, recv_sems.at[recv]).wait()
@@ -103,8 +108,11 @@
     barrier = pltpu.get_barrier_semaphore()
     for k in range(1, count):
         pl.semaphore_signal(barrier, inc=1, device_id={"seq": (me + k) % count}, device_id_type=MESH)
+    codes_ref[...] = jnp.broadcast_to(bases_ref[...], codes_ref.shape)
     cot_t[...] = jnp.transpose(cot_ref[...])
-    hid[...] = jnp.zeros_like(hid)
+    for g in range(GROUPS):
+        edges[0, g] = cot_ref[0:16, cg * g : cg * (g + 1)]
+        edges[1, g] = cot_ref[band - 16 :, cg * g : cg * (g + 1)]
     pl.semaphore_wait(barrier, count - 1)
 
     place = pl.ds(pl.multiple_of(band_of * band, LANES), band)
@@ -124,10 +132,34 @@
             push(second_ref, second_all.at[member], 3, 4, group * members + k)
     for g in range(GROUPS):
         push(cot_t.at[pl.ds(cg * g, cg)], cot_in.at[:, place], 4, 5, g * members + chunk_of)
-    push_edges(
-        lambda g, low: cot_t.at[pl.ds(cg * g, cg), pl.ds(0 if low else band - LANES, LANES)],
-        cot_left, cot_right, 5, 6, 7,
-    )
+    push_edges(lambda g, low: edges.at[0 if low else 1, g], cot_left, cot_right, 5, 6, 7)
+
+    channels = GROUPS * cg
+    row = lax.broadcasted_iota(jnp.int32, (16, channels), 0)
+    lane = lax.broadcasted_iota(jnp.int32, (16, channels), 1)
+    code = jnp.where(row < 8, row & 3, 3 - (row & 3))
+    table = table_ref[...].astype(F32)
+    wide = jnp.zeros((16, channels), F32)
+    for c in range(4):
+        wide = jnp.where(code == c, table[c : c + 1], wide)
+    wide = jnp.where(lane < cg, pltpu.roll(wide, (channels - group * cg) % channels, 1), 0.0)
+    wide = jnp.concatenate([wide, jnp.zeros((16, LANES), F32)], axis=1)
+    eye = (
+        lax.broadcasted_iota(jnp.int32, (cg, cg), 0) == lax.broadcasted_iota(jnp.int32, (cg, cg), 1)
+    ).astype(F32).astype(BF16)
+    for s in range(2):
+        strand = wide[8 * s : 8 * (s + 1)]
+        diag_ref[s] = jnp.concatenate(
+            [pltpu.roll(strand, cg * (u if s == 0 else TAPS - 1 - u), 1) for u in range(TAPS)], axis=0
+        )[:, : TAPS * cg].astype(BF16)
+        own = jnp.where(lax.broadcasted_iota(jnp.int32, (8, cg), 0) < 4, strand[:, :cg], 0.0)
+        blank = jnp.zeros((8 * HALF, cg), F32)
+        skip_ref[s] = lane_contract(
+            eye, jnp.concatenate([blank, own, blank], axis=0).astype(BF16)
+        ).astype(BF16)
+    pltpu.make_async_copy(diag_ref, diag_out, diag_sem).start()
+    for top in (cg, HIGH + cg):
+        hid[top : top + HIGH - cg, :] = jnp.zeros((HIGH - cg, width), BF16)
 
     has_right = (member < members - 1).astype(jnp.int32)
     has_left = (member > 0).astype(jnp.int32)
@@ -195,15 +227,29 @@
         out_r = jnp.dot(second, unf_r[:, cols], preferred_element_type=F32)
         out_r += jnp.dot(skip_ref[1], onehot[:, cols], preferred_element_type=F32)
         comb_send[:, cols] = (out_f + out_r.astype(BF16).astype(F32)).astype(BF16)
+        for k in range(step // band):
+            j = i * (step // band) + k
+            push(
+                comb_send.at[:, pl.ds(pl.multiple_of(j * band, LANES), band)], comb_in.at[group],
+                6, 8, member * GROUPS + j, keep=False,
+            )
 
     for j in range(GROUPS):
-        push(comb_send.at[:, pl.ds(j * band, band)], comb_in.at[group], 6, 8, member * GROUPS + j)
+        keep_for_send(
+            comb_send.at[:, pl.ds(j * band, band)], comb_in.at[group], 6, 8, member * GROUPS + j
+        )
 
     arrived(cot_in, 5)
     edges_arrived(cot_left, cot_right, 6, 7)
-    on_right, real = edge_mask(cg)
-    edge = jnp.where(
-        real, jnp.where(on_right, cot_right[...].astype(F32), cot_left[...].astype(F32)), 0.0
+    edge = jnp.transpose(
+        jnp.concatenate(
+            [
+                jnp.where(has_right > 0, cot_right[...].astype(F32), 0.0),
+                jnp.zeros((LANES - 32, cg), F32),
+                jnp.where(has_left > 0, cot_left[...].astype(F32), 0.0),
+            ],
+            axis=0,
+        )
     ).astype(BF16)
     cot = jnp.concatenate([cot_in[...], edge], axis=1)
     for t in range(TAPS):
@@ -221,14 +267,13 @@
             s_acc[cg * (TAPS - 1 - t) : cg * (TAPS - t), 0:cg]
             + s_acc[cg * t : cg * (t + 1), HIGH : HIGH + cg]
         )
-        if gathered:
-            second_out[t] = block
-        else:
-            for k in range(members):
-                s_send[k, t] = block[rows * k : rows * (k + 1)]
-    if not gathered:
+        for k in range(members if not gathered else 1):
+            s_send[k, t] = block[s_rows * k : s_rows * (k + 1)]
+    if gathered:
+        pltpu.make_async_copy(s_send.at[0], second_out.at[0], recv_sems.at[9]).start()
+    else:
         for k in range(members):
-            push(s_send.at[k], s_in.at[member], 7, 9, group * members + k)
+            push(s_send.at[k], second_out.at[member], 7, 9, group * members + k)
 
     turned = jnp.transpose(second)
     for u in range(TAPS):
@@ -245,31 +290,35 @@
         return total + lane_contract(pre_grad, onehot[:, cols])
 
     terms = lax.fori_loop(0, chunk // step, backward, jnp.zeros((2 * cg, 8 * TAPS), F32))
+    for k in range(members if not gathered else 1):
+        for s in range(2):
+            g_send[k, s] = terms[s * cg + s_rows * k : s * cg + s_rows * (k + 1)]
     if gathered:
-        first_out[0] = terms[:cg]
-        first_out[1] = terms[cg:]
+        pltpu.make_async_copy(g_send.at[0], first_out.at[0], recv_sems.at[10]).start()
     else:
         for k in range(members):
-            for s in range(2):
-                g_send[k, s] = terms[s * cg + rows * k : s * cg + rows * (k + 1)]
-        for k in range(members):
-            push(g_send.at[k], g_in.at[member], 8, 10, group * members + k)
-
+            push(g_send.at[k], first_out.at[member], 8, 10, group * members + k)
+
+    pltpu.make_async_copy(diag_ref, diag_out, diag_sem).wait()
     arrived(comb_in, 8)
-    comb_ref[...] = jnp.transpose(comb_in[...].reshape(GROUPS * cg, band))
-    if not gathered:
-        arrived(s_in, 9)
-        second_out[...] = jnp.sum(s_in[...], axis=0)
-        arrived(g_in, 10)
-        summed = jnp.sum(g_in[...], axis=0)
-        first_out[...] = jnp.dot(
-            split_halves(summed[0], 1), diag_ref[0], preferred_element_type=F32
-        ) + jnp.dot(split_halves(summed[1], 1), diag_ref[1], preferred_element_type=F32)
-
+    arrived(second_out, 9)
+    arrived(first_out, 10)
     for remote, target, here in started:
         @pl.when((target != me) if here is None else (here & (target != me)))
         def _():
             remote.wait_send()
+
+
+def finish_kernel(comb_in, first_in, second_in, diag_ref, comb_ref, first_ref, second_ref):
+    taps, _, cg = second_in.shape[1:]
+    comb_ref[...] = jnp.transpose(comb_in[...].reshape(comb_in.shape[0] * cg, comb_in.shape[2]))
+    summed = jnp.sum(second_in[...], axis=0)
+    for t in range(taps):
+        second_ref[:, cg * t : cg * (t + 1)] = summed[t]
+    terms = jnp.sum(first_in[...], axis=0)
+    first_ref[...] = jnp.dot(
+        split_halves(terms[0], 1), diag_ref[0], preferred_element_type=F32
+    ) + jnp.dot(split_halves(terms[1], 1), diag_ref[1], preferred_element_type=F32)
 
 
 def per_device(bases, base_table, first_kernel, second_kernel, cotangent):
@@ -281,53 +330,40 @@
     chunk = band * GROUPS
     width = chunk + LANES
     step = math.gcd(chunk, 512)
-    me = lax.axis_index("seq")
     gathered = rows % 16 != 0
 
-    table = lax.dynamic_slice_in_dim(base_table, (me // members) * cg, cg, axis=1)
     columns = 8 * TAPS
-    offset = jnp.arange(columns) // 8
-    high = jnp.arange(columns) % 8 < 4
-    tap = jnp.arange(TAPS * cg) // cg
-    zero = jnp.zeros((), BF16)
-    diag, skip = [], []
-    for s in range(2):
-        strand = table if s == 0 else table[::-1]
-        wanted = offset if s == 0 else TAPS - 1 - offset
-        diag.append(jnp.where(wanted[:, None] == tap[None, :], jnp.tile(strand, (2 * TAPS, TAPS)), zero))
-        chosen = ((offset == HALF) & high)[None, :]
-        skip.append(jnp.where(chosen, jnp.tile(strand.T, (1, 2 * TAPS)), zero))
-    diag, skip = jnp.stack(diag), jnp.stack(skip)
-    codes = jnp.broadcast_to(bases[None, :], (8, band))
-
     if gathered:
         same = [[g * members + k for k in range(members)] for g in range(GROUPS)]
         first_kernel = lax.all_gather(first_kernel, "seq", axis=0, tiled=True, axis_index_groups=same)
         second_kernel = lax.all_gather(second_kernel, "seq", axis=0, tiled=True, axis_index_groups=same)
-        outs = ((2, cg, columns), (TAPS, cg, cg))
-        lot, lot_rows = 1, 16
+        lot, lot_rows = 1, cg
     else:
-        outs = ((rows, TAPS * cg), (TAPS, rows, cg))
         lot, lot_rows = members, rows
 
     vmem = pltpu.VMEM
-    combined, first_grad, second_grad = pl.pallas_call(
+    comb_parts, first_parts, second_parts, diag = pl.pallas_call(
         functools.partial(block_kernel, count, members, gathered, step),
         out_shape=(
-            jax.ShapeDtypeStruct((band, channels), BF16),
-            jax.ShapeDtypeStruct(outs[0], F32),
-            jax.ShapeDtypeStruct(outs[1], F32),
+            jax.ShapeDtypeStruct((GROUPS, cg, band), BF16),
+            jax.ShapeDtypeStruct((lot, 2, lot_rows, columns), F32),
+            jax.ShapeDtypeStruct((lot, TAPS, lot_rows, cg), F32),
+            jax.ShapeDtypeStruct((2, columns, TAPS * cg), BF16),
         ),
-        in_specs=[pl.BlockSpec(memory_space=vmem)] * 6,
-        out_specs=[pl.BlockSpec(memory_space=vmem)] * 3,
+        in_specs=[pl.BlockSpec(memory_space=vmem)] * 5,
+        out_specs=[pl.BlockSpec(memory_space=pl.ANY)] * 4,
         scratch_shapes=[
+            vmem((2, columns, TAPS * cg), BF16),
+            vmem((2, cg, columns), BF16),
+            vmem((2, GROUPS, 16, cg), BF16),
+            vmem((8, band), jnp.int32),
             vmem((channels, band), BF16),
             vmem((8, chunk), jnp.int32),
             vmem((8, LANES), jnp.int32),
             vmem((8, LANES), jnp.int32),
             vmem((cg, chunk), BF16),
-            vmem((cg, LANES), BF16),
-            vmem((cg, LANES), BF16),
+            vmem((16, cg), BF16),
+            vmem((16, cg), BF16),
             vmem((lot, lot_rows, TAPS * cg), BF16),
             vmem((lot, lot_rows, TAPS * cg), BF16),
             vmem((columns, width), BF16),
@@ -339,34 +375,33 @@
             vmem((TAPS, 2 * cg, cg), BF16),
             vmem((TAPS * cg, 2 * HIGH), F32),
             vmem((cg, chunk), BF16),
-            vmem((GROUPS, cg, band), BF16),
             vmem((lot, TAPS, lot_rows, cg), F32),
-            vmem((lot, TAPS, lot_rows, cg), F32),
-            vmem((lot, 2, lot_rows, columns), F32),
             vmem((lot, 2, lot_rows, columns), F32),
             pltpu.SemaphoreType.DMA((9,)),
             pltpu.SemaphoreType.DMA((11,)),
+            pltpu.SemaphoreType.DMA,
         ],
         compiler_params=pltpu.CompilerParams(
             collective_id=0, has_side_effects=True, vmem_limit_bytes=56 * 1024 * 1024
         ),
-    )(codes, diag, skip, first_kernel, second_kernel, cotangent)
-
+    )(bases.reshape(1, band), base_table, first_kernel, second_kernel, cotangent)
+
+    finished = pl.pallas_call(
+        finish_kernel,
+        out_shape=(
+            jax.ShapeDtypeStruct((band, channels), BF16),
+            jax.ShapeDtypeStruct((lot_rows, TAPS * cg), F32),
+            jax.ShapeDtypeStruct((lot_rows, TAPS * cg), F32),
+        ),
+        in_specs=[pl.BlockSpec(memory_space=vmem)] * 4,
+        out_specs=[pl.BlockSpec(memory_space=vmem)] * 3,
+    )(comb_parts, first_parts, second_parts, diag)
     if gathered:
-        first_local = jnp.zeros((cg, TAPS * cg), F32)
-        for s in range(2):
-            first_local += jnp.einsum(
-                "oc,ck->ok",
-                jnp.where(high[None, :], first_grad[s], 0.0),
-                diag[s].astype(F32),
-                precision=lax.Precision.HIGHEST,
-            )
-        second_local = jnp.transpose(second_grad, (1, 0, 2)).reshape(cg, TAPS * cg)
         scatter = functools.partial(
             lax.psum_scatter, axis_name="seq", scatter_dimension=0, tiled=True, axis_index_groups=same
         )
-        return combined, scatter(first_local), scatter(second_local)
-    return combined, first_grad, jnp.transpose(second_grad, (1, 0, 2)).reshape(rows, TAPS * cg)
+        return finished[0], scatter(finished[1]), scatter(finished[2])
+    return tuple(finished)
 
 
 def solution(mesh):

time: 38.5 us -> 31.2 us (0.81)
  local copies, waits for them, and re-layouts: 6.58 us -> 0 us
  other arithmetic: 1.54 us -> 0 us
  Pallas kernels: 29.3 us -> 30 us
    unnamed x10 -> x0, local copies, waits for them, and re-layouts: 3.25 us -> none
    pallas_call x0 -> x1, Pallas kernels: none -> 2.29 us  [per_device(): pl.pallas_call(finish_kernel, out_shape=(jax.ShapeDtypeStruct((band, chan...]
    pallas_call x1, Pallas kernels: 29.3 us -> 27.8 us  [per_device(): pl.pallas_call(functools.partial(block_kernel, count, members, gathered,...]
    another operation x2 -> x0, other arithmetic: 1.37 us -> none  [per_device(): diag, skip = (jnp.stack(diag), jnp.stack(skip))]
    transpose x2 -> x0, local copies, waits for them, and re-layouts: 1.1 us -> none  [the longest x1 1.02 us: per_device(): jnp.transpose(second_grad, (1, 0, 2)).reshape(rows, TAPS * cg)]
    reshape x1 -> x0, local copies, waits for them, and re-layouts: 0.79 us -> none  [per_device(): jnp.transpose(second_grad, (1, 0, 2)).reshape(rows, TAPS * cg)]
    another operation x8 -> x0, local copies, waits for them, and re-layouts: 0.74 us -> none  [the longest x4 0.52 us: per_device(): jnp.tile(strand, (2 * TAPS, TAPS))]
    broadcast_in_dim x1 -> x0, local copies, waits for them, and re-layouts: 0.6 us -> none  [per_device(): codes = jnp.broadcast_to(bases[None, :], (8, band))]
where the time goes in v2:
time: 31.2 us; the launch traced here: 30.7 us
  Pallas kernels  30 us (96%)
  between operations  0.64 us (2%)
    pallas_call x1, Pallas kernels, per_device(): pl.pallas_call(functools.partial(block_kernel, count, members, gathered,...  27.8 us
    pallas_call x1, Pallas kernels, per_device(): pl.pallas_call(finish_kernel, out_shape=(jax.ShapeDtypeStruct((band, chan...  2.29 us

profile of v2, /device:TPU:1, one launch (start us, length us, event | category | flops | bytes accessed | tf_op | source)
XLA Modules:
  0.0 30.7 jit_solution(2634433904551100210)
XLA Ops:
  0.6 27.8 %shard_map.76 = (bf16[8,96,256]{2,1,0:T(8,128)(2,1)}, f32[2,2,48,72]{3,2,1,0:T(8,128)}, f32[2,9,48,96]{3,2,1,0:T(8,128)}, bf16[2,72,864]{2,1,0:T(8,128)(2,1)}) custom-call(s32[1,256]{1,0:T(1,128)} %bitcast.1, bf16[4,768]{1,0:T(4,128)(2,1)} %table_ref.1, bf16[48,864]{1,0:T(8,128)(2,1)} %first_ref.1, bf16[48,864]{1,0:T(8,128)(2,1)} %second_ref.1, ...), custom_call_target="tpu_custom_call" | custom-call | tf_op jit(solution)/shard_map/pallas_call | solution.py:345
  28.4 2.3 %shard_map.77 = (bf16[256,768]{1,0:T(8,128)(2,1)}, f32[48,864]{1,0:T(8,128)}, f32[48,864]{1,0:T(8,128)}) custom-call(bf16[8,96,256]{2,1,0:T(8,128)(2,1)} %get-tuple-element.7.comb_in, f32[2,2,48,72]{3,2,1,0:T(8,128)} %get-tuple-element.8.first_in, f32[2,9,48,96]{3,2,1,0:T(8,128)} %get-tuple-element.9.second_in, bf16[2,72,864]{2,1,0:T(8,128)(2,1)} %get-tuple-element.10.diag_ref), custom_call_target="tpu_custom_call" | custom-call | tf_op jit(solution)/shard_map/pallas_call | solution.py:389

commit v3 on v2

--- a/solution.py
+++ b/solution.py
@@ -32,16 +32,16 @@
     count, members, gathered, step,
     bases_ref, table_ref, first_ref, second_ref, cot_ref,
     comb_in, first_out, second_out, diag_out,
-    diag_ref, skip_ref, edges, codes_ref, cot_t, codes_in, codes_left, codes_right, cot_in, cot_left, cot_right,
+    diag_ref, diag_own, skip_ref, edges, codes_ref, cot_t, codes_in, codes_left, codes_right, cot_in, cot_left, cot_right,
     first_all, second_all, onehot, hid, slope, unf_f, unf_r, cot_unf, adj,
     s_acc, comb_send, s_send, g_send,
     send_sems, recv_sems, diag_sem,
 ):
     me = lax.axis_index("seq")
-    group = me // members
-    member = me % members
-    chunk_of = me // GROUPS
-    band_of = me % GROUPS
+    group = me % GROUPS
+    member = me // GROUPS
+    band_of = group
+    owned, piece = me // members, me % members
     band = cot_ref.shape[0]
     chunk = band * GROUPS
     width = chunk + LANES
@@ -75,12 +75,12 @@
 
     def push_edges(src_of, left_dst, right_dst, kind, recv_left, recv_right):
         for low, dst, recv, here, there in (
-            (True, right_dst, recv_right, (band_of == 0) & (chunk_of > 0), chunk_of - 1),
-            (False, left_dst, recv_left, (band_of == GROUPS - 1) & (chunk_of < members - 1), chunk_of + 1),
+            (True, right_dst, recv_right, (band_of == 0) & (member > 0), member - 1),
+            (False, left_dst, recv_left, (band_of == GROUPS - 1) & (member < members - 1), member + 1),
         ):
             for g in range(GROUPS):
                 src = src_of(g, low)
-                target = g * members + there
+                target = there * GROUPS + g
                 remote = pltpu.make_async_remote_copy(
                     src_ref=src, dst_ref=dst, send_sem=send_sems.at[kind], recv_sem=recv_sems.at[recv],
                     device_id={"seq": target}, device_id_type=MESH,
@@ -117,7 +117,7 @@
 
     place = pl.ds(pl.multiple_of(band_of * band, LANES), band)
     for g in range(GROUPS):
-        push(codes_ref, codes_in.at[:, place], 0, 0, g * members + chunk_of)
+        push(codes_ref, codes_in.at[:, place], 0, 0, member * GROUPS + g)
     push_edges(
         lambda g, low: codes_ref.at[:, pl.ds(0 if low else band - LANES, LANES)],
         codes_left, codes_right, 1, 1, 2,
@@ -127,37 +127,44 @@
         second = second_ref[...]
     else:
         for k in range(members):
-            push(first_ref, first_all.at[member], 2, 3, group * members + k)
+            push(first_ref, first_all.at[piece], 2, 3, k * GROUPS + owned)
         for k in range(members):
-            push(second_ref, second_all.at[member], 3, 4, group * members + k)
+            push(second_ref, second_all.at[piece], 3, 4, k * GROUPS + owned)
     for g in range(GROUPS):
-        push(cot_t.at[pl.ds(cg * g, cg)], cot_in.at[:, place], 4, 5, g * members + chunk_of)
+        push(cot_t.at[pl.ds(cg * g, cg)], cot_in.at[:, place], 4, 5, member * GROUPS + g)
     push_edges(lambda g, low: edges.at[0 if low else 1, g], cot_left, cot_right, 5, 6, 7)
 
     channels = GROUPS * cg
-    row = lax.broadcasted_iota(jnp.int32, (16, channels), 0)
-    lane = lax.broadcasted_iota(jnp.int32, (16, channels), 1)
-    code = jnp.where(row < 8, row & 3, 3 - (row & 3))
-    table = table_ref[...].astype(F32)
-    wide = jnp.zeros((16, channels), F32)
-    for c in range(4):
-        wide = jnp.where(code == c, table[c : c + 1], wide)
-    wide = jnp.where(lane < cg, pltpu.roll(wide, (channels - group * cg) % channels, 1), 0.0)
-    wide = jnp.concatenate([wide, jnp.zeros((16, LANES), F32)], axis=1)
+
+    def group_table(of_group):
+        row = lax.broadcasted_iota(jnp.int32, (16, channels), 0)
+        lane = lax.broadcasted_iota(jnp.int32, (16, channels), 1)
+        code = jnp.where(row < 8, row & 3, 3 - (row & 3))
+        table = table_ref[...].astype(F32)
+        wide = jnp.zeros((16, channels), F32)
+        for c in range(4):
+            wide = jnp.where(code == c, table[c : c + 1], wide)
+        shift = (channels - of_group * cg) % channels
+        wide = jnp.where(lane < cg, pltpu.roll(wide, shift, 1), 0.0)
+        return jnp.concatenate([wide, jnp.zeros((16, LANES), F32)], axis=1)
+
+    def spread(strand, s):
+        return jnp.concatenate(
+            [pltpu.roll(strand, cg * (u if s == 0 else TAPS - 1 - u), 1) for u in range(TAPS)], axis=0
+        )[:, : TAPS * cg].astype(BF16)
+
+    wide = group_table(group)
     eye = (
         lax.broadcasted_iota(jnp.int32, (cg, cg), 0) == lax.broadcasted_iota(jnp.int32, (cg, cg), 1)
     ).astype(F32).astype(BF16)
     for s in range(2):
         strand = wide[8 * s : 8 * (s + 1)]
-        diag_ref[s] = jnp.concatenate(
-            [pltpu.roll(strand, cg * (u if s == 0 else TAPS - 1 - u), 1) for u in range(TAPS)], axis=0
-        )[:, : TAPS * cg].astype(BF16)
+        diag_ref[s] = spread(strand, s)
         own = jnp.where(lax.broadcasted_iota(jnp.int32, (8, cg), 0) < 4, strand[:, :cg], 0.0)
         blank = jnp.zeros((8 * HALF, cg), F32)
         skip_ref[s] = lane_contract(
             eye, jnp.concatenate([blank, own, blank], axis=0).astype(BF16)
         ).astype(BF16)
-    pltpu.make_async_copy(diag_ref, diag_out, diag_sem).start()
     for top in (cg, HIGH + cg):
         hid[top : top + HIGH - cg, :] = jnp.zeros((HIGH - cg, width), BF16)
 
@@ -194,9 +201,9 @@
         cdf = 0.5 + 0.5 * lax.erf(pre * math.sqrt(0.5))
         return pre * cdf, cdf + pre * jnp.exp(-0.5 * pre * pre) * (1.0 / math.sqrt(2.0 * math.pi))
 
-    @pl.loop(0, chunk // 256)
+    @pl.loop(0, chunk // step)
     def _(i):
-        cols = pl.ds(pl.multiple_of(i * 256, 256), 256)
+        cols = pl.ds(pl.multiple_of(i * step, step), step)
         hidden, grad = activate(cols)
         hidden = hidden.astype(BF16)
         hid[0:cg, cols] = hidden[:cg]
@@ -255,12 +262,7 @@
     for t in range(TAPS):
         cot_unf[cg * t : cg * (t + 1), :] = pltpu.roll(cot, (HALF - t) % width, 1)[:, :chunk]
 
-    s_acc[...] = jnp.zeros_like(s_acc)
-
-    @pl.loop(0, chunk // step)
-    def _(i):
-        cols = pl.ds(pl.multiple_of(i * step, step), step)
-        s_acc[...] += lane_contract(cot_unf[:, cols], hid[:, cols])
+    s_acc[...] = lane_contract(cot_unf[...], hid[:, :chunk])
 
     for t in range(TAPS):
         block = (
@@ -275,21 +277,21 @@
         for k in range(members):
             push(s_send.at[k], second_out.at[member], 7, 9, group * members + k)
 
+    wide = group_table(group if gathered else owned)
+    for s in range(2):
+        diag_own[s] = spread(wide[8 * s : 8 * (s + 1)], s)
+    pltpu.make_async_copy(diag_own, diag_out, diag_sem).start()
+
     turned = jnp.transpose(second)
     for u in range(TAPS):
         v = TAPS - 1 - u
         adj[u, 0:cg] = turned[cg * v : cg * (v + 1)]
         adj[u, cg:] = turned[cg * u : cg * (u + 1)]
 
-    def backward(i, total):
-        cols = pl.ds(pl.multiple_of(i * step, step), step)
-        grad = jnp.dot(adj[0], cot_unf[0:cg, cols], preferred_element_type=F32)
-        for u in range(1, TAPS):
-            grad += jnp.dot(adj[u], cot_unf[cg * u : cg * (u + 1), cols], preferred_element_type=F32)
-        pre_grad = (grad * slope[:, cols]).astype(BF16)
-        return total + lane_contract(pre_grad, onehot[:, cols])
-
-    terms = lax.fori_loop(0, chunk // step, backward, jnp.zeros((2 * cg, 8 * TAPS), F32))
+    grad = jnp.dot(adj[0], cot_unf[0:cg, :], preferred_element_type=F32)
+    for u in range(1, TAPS):
+        grad += jnp.dot(adj[u], cot_unf[cg * u : cg * (u + 1), :], preferred_element_type=F32)
+    terms = lane_contract((grad * slope[...]).astype(BF16), onehot[:, :chunk])
     for k in range(members if not gathered else 1):
         for s in range(2):
             g_send[k, s] = terms[s * cg + s_rows * k : s * cg + s_rows * (k + 1)]
@@ -299,7 +301,7 @@
         for k in range(members):
             push(g_send.at[k], first_out.at[member], 8, 10, group * members + k)
 
-    pltpu.make_async_copy(diag_ref, diag_out, diag_sem).wait()
+    pltpu.make_async_copy(diag_own, diag_out, diag_sem).wait()
     arrived(comb_in, 8)
     arrived(second_out, 9)
     arrived(first_out, 10)
@@ -334,9 +336,13 @@
 
     columns = 8 * TAPS
     if gathered:
-        same = [[g * members + k for k in range(members)] for g in range(GROUPS)]
-        first_kernel = lax.all_gather(first_kernel, "seq", axis=0, tiled=True, axis_index_groups=same)
-        second_kernel = lax.all_gather(second_kernel, "seq", axis=0, tiled=True, axis_index_groups=same)
+        group = lax.axis_index("seq") % GROUPS
+        first_kernel, second_kernel = (
+            lax.dynamic_slice_in_dim(
+                lax.all_gather(kernel, "seq", axis=0, tiled=True), group * cg, cg, axis=0
+            )
+            for kernel in (first_kernel, second_kernel)
+        )
         lot, lot_rows = 1, cg
     else:
         lot, lot_rows = members, rows
@@ -353,6 +359,7 @@
         in_specs=[pl.BlockSpec(memory_space=vmem)] * 5,
         out_specs=[pl.BlockSpec(memory_space=pl.ANY)] * 4,
         scratch_shapes=[
+            vmem((2, columns, TAPS * cg), BF16),
             vmem((2, columns, TAPS * cg), BF16),
             vmem((2, cg, columns), BF16),
             vmem((2, GROUPS, 16, cg), BF16),
@@ -397,10 +404,15 @@
         out_specs=[pl.BlockSpec(memory_space=vmem)] * 3,
     )(comb_parts, first_parts, second_parts, diag)
     if gathered:
-        scatter = functools.partial(
-            lax.psum_scatter, axis_name="seq", scatter_dimension=0, tiled=True, axis_index_groups=same
-        )
-        return finished[0], scatter(finished[1]), scatter(finished[2])
+        blank = jnp.zeros((channels, TAPS * cg), F32)
+        first_grad, second_grad = (
+            lax.psum_scatter(
+                lax.dynamic_update_slice_in_dim(blank, grad, group * cg, axis=0),
+                "seq", scatter_dimension=0, tiled=True,
+            )
+            for grad in finished[1:]
+        )
+        return finished[0], first_grad, second_grad
     return tuple(finished)
 
 

time: 31.2 us -> 38 us (1.22)
  Pallas kernels: 30 us -> 37 us
    pallas_call x1, Pallas kernels: 27.8 us -> 34.7 us  [per_device(): pl.pallas_call(functools.partial(block_kernel, count, members, gathered,...]
where the time goes in v3:
time: 38 us; the launch traced here: 37.7 us
  Pallas kernels  37 us (97%)
  between operations  0.64 us (2%)
    pallas_call x1, Pallas kernels, per_device(): pl.pallas_call(functools.partial(block_kernel, count, members, gathered,...  34.7 us
    pallas_call x1, Pallas kernels, per_device(): pl.pallas_call(finish_kernel, out_shape=(jax.ShapeDtypeStruct((band, chan...  2.29 us

profile of v3, /device:TPU:1, one launch (start us, length us, event | category | flops | bytes accessed | tf_op | source)
XLA Modules:
  0.0 37.7 jit_solution(2496681696342676755)
XLA Ops:
  0.6 34.7 %shard_map.76 = (bf16[8,96,256]{2,1,0:T(8,128)(2,1)}, f32[2,2,48,72]{3,2,1,0:T(8,128)}, f32[2,9,48,96]{3,2,1,0:T(8,128)}, bf16[2,72,864]{2,1,0:T(8,128)(2,1)}) custom-call(s32[1,256]{1,0:T(1,128)} %bitcast.1, bf16[4,768]{1,0:T(4,128)(2,1)} %table_ref.1, bf16[48,864]{1,0:T(8,128)(2,1)} %first_ref.1, bf16[48,864]{1,0:T(8,128)(2,1)} %second_ref.1, ...), custom_call_target="tpu_custom_call" | custom-call | tf_op jit(solution)/shard_map/pallas_call | solution.py:351
  35.4 2.3 %shard_map.77 = (bf16[256,768]{1,0:T(8,128)(2,1)}, f32[48,864]{1,0:T(8,128)}, f32[48,864]{1,0:T(8,128)}) custom-call(bf16[8,96,256]{2,1,0:T(8,128)(2,1)} %get-tuple-element.7.comb_in, f32[2,2,48,72]{3,2,1,0:T(8,128)} %get-tuple-element.8.first_in, f32[2,9,48,96]{3,2,1,0:T(8,128)} %get-tuple-element.9.second_in, bf16[2,72,864]{2,1,0:T(8,128)(2,1)} %get-tuple-element.10.diag_ref), custom_call_target="tpu_custom_call" | custom-call | tf_op jit(solution)/shard_map/pallas_call | solution.py:396
